TPU v7x, 32 devices: a whole 2x2x4 slice. The times are simulated.
32 devices in a mesh: gx: 16 (over z, y, x), gy: 2 (over core).
Axes of the slice: x: 2, y: 2, z: 4, core: 2. Of those that a mesh axis runs over, the one named last changes fastest.
Arguments:
- density: float32 [128, 32, 64], P('gx', None, 'gy'), may hold values from 0.5 to 1.5
- momentum: float32 [3, 128, 32, 64], P(None, 'gx', None, 'gy'), may hold values from -3 to 3
- energy: float32 [128, 32, 64], P('gx', None, 'gy'), may hold values from 2.5 to 4
- eddy_normal_cell: int32 [1024], P('gx'), may hold values from 0 to 63
- eddy_spanwise_cell: int32 [1024], P('gx'), may hold values from 0 to 31
- eddy_signs: int32 [1024, 3], P('gx'), may hold values from 0 to 1
- eddy_strengths: float32 [1024], P('gx'), may hold values from 0.3 to 3
- filter_matrices: float32 [1, 128, 128], replicated, may hold values from -1.25 to 1.25
- shock_switch: int32 [1, 64], P(None, 'gy'), may hold values 0 or 1
- dilatation_bin: int32 [128, 32, 64], P('gx', None, 'gy'), may hold values from 0 to 63
- vorticity_bin: int32 [128, 32, 64], P('gx', None, 'gy'), may hold values from 0 to 63, as said below
Outputs:
- conserved_next: float32 [5, 128, 32, 64], P(None, 'gx', None, 'gy')
- histogram: float32 [64, 64], replicated
Inputs may be any that keep to these rules, and one draw needn't show every extreme that they name: vorticity_bin at streamwise cell x is x * 64 // 128 or one more, modulo 64.
All inputs are finite; a program needn't handle non-finite values. No bound on the sum of `shock_switch` on one device may be relied on, other than what follows from the above.
Results may differ from a plain program's by a relative error of at most 0.0003.
Values sent between devices are 32-bit elements; how exact they have to be, the bound alone decides.
No kernel may reach another device: no remote copies, remote signals or barrier semaphores. Data moves between devices by JAX's collectives and lax.ppermute only.
A program may use at most 64 MiB of HBM per device.

v0:
```python
import math
import jax
import jax.numpy as jnp
from jax import lax
from jax.sharding import PartitionSpec as P

HISTOGRAM_BINS = 64
SIGMA_Y = 32
SIGMA_Z = 8
TIME_STEP = 0.1
GAMMA_GAS = 1.4
SENSOR_EPS = 0.1
HAT_PEAK = math.sqrt(1.5)


def extended(x, sides, width):
    for axis, dim in sides:
        size, length = (lax.axis_size(axis), x.shape[dim])
        up = [(i, (i + 1) % size) for i in range(size - 1)]
        down = [(j, i) for i, j in up]
        last = lax.slice_in_dim(x, length - width, length, axis=dim)
        first = lax.slice_in_dim(x, 0, width, axis=dim)
        before = lax.ppermute(last, axis, up)
        after = lax.ppermute(first, axis, down)
        x = jnp.concatenate([before, x, after], axis=dim)
    return x


def hat_shape(centres, coords, spread, period):
    offset = coords[None, :] - centres[:, None]
    if period > 0:
        offset = jnp.mod(offset + period / 2, period) - period / 2
    return HAT_PEAK * jnp.maximum(0.0, 1.0 - jnp.abs(offset) / spread)


def inflow_from(centre_y, centre_z, eddy_weight, coords_y, coords_z, span):
    shape_y = hat_shape(centre_y, coords_y, float(SIGMA_Y), 0)
    shape_z = hat_shape(centre_z, coords_z, float(SIGMA_Z), span)
    weighted = (eddy_weight[:, :, None] * shape_z[:, None, :]).reshape(eddy_weight.shape[0], -1)
    inflow = jnp.dot(weighted.T, shape_y, precision=lax.Precision.HIGHEST)
    return inflow.reshape(3, coords_z.shape[0], coords_y.shape[0])


def ghost_state(inflow):
    mom_x = 1.0 + inflow[0]
    kinetic = mom_x * mom_x + inflow[1] * inflow[1] + inflow[2] * inflow[2]
    return jnp.stack([jnp.ones_like(mom_x), mom_x, inflow[1], inflow[2], 3.0 + 0.5 * kinetic])


def flux_of(fields, velocity, pressure, direction):
    result = fields * velocity[direction][None]
    result = result.at[1 + direction].add(pressure)
    return result.at[4].add(pressure * velocity[direction])


def central_x(values):
    return (values[..., 2:, :, 1:-1] - values[..., :-2, :, 1:-1]) * 0.5


def central_y(values):
    return (values[..., 1:-1, :, 2:] - values[..., 1:-1, :, :-2]) * 0.5


def central_z(values):
    centre = values[..., 1:-1, :, 1:-1]
    return (jnp.roll(centre, -1, axis=-2) - jnp.roll(centre, 1, axis=-2)) * 0.5


def section_rhs(padded):
    velocity = padded[1:4] / padded[0][None]
    pressure = (GAMMA_GAS - 1.0) * (padded[4] - 0.5 * jnp.sum(padded[1:4] * velocity, axis=0))
    change = central_x(flux_of(padded, velocity, pressure, 0))
    change = change + central_y(flux_of(padded, velocity, pressure, 1))
    change = change + central_z(flux_of(padded, velocity, pressure, 2))
    updated = padded[:, 1:-1, :, 1:-1] - TIME_STEP * change
    dilatation = central_x(velocity[0]) + central_y(velocity[1]) + central_z(velocity[2])
    vort_x = central_y(velocity[2]) - central_z(velocity[1])
    vort_y = central_z(velocity[0]) - central_x(velocity[2])
    vort_z = central_x(velocity[1]) - central_y(velocity[0])
    squared = dilatation * dilatation
    shock_sensor = squared / (
        squared + vort_x * vort_x + vort_y * vort_y + vort_z * vort_z + SENSOR_EPS
    )
    return (updated, shock_sensor)


def filter_lines(pencil, filter_matrices):
    block_count, block_len = (filter_matrices.shape[0], filter_matrices.shape[1])
    lanes = pencil.shape[2]
    blocks = pencil.reshape(5, block_count, block_len, lanes)
    smooth = jnp.einsum("bij,fbjp->fbip", filter_matrices, blocks, precision=lax.Precision.HIGHEST)
    return smooth.reshape(5, block_count * block_len, lanes)


def plane_histogram(shock_sensor, dilatation_bin, vorticity_bin):
    bin_levels = jnp.arange(HISTOGRAM_BINS, dtype=jnp.int32)

    def accumulate_plane(histogram_totals, histogram_parts):
        sensor_plane, plane_dilatation, plane_vorticity = histogram_parts
        flat_sensor = sensor_plane.reshape(-1)
        dilatation_table = (plane_dilatation.reshape(-1)[None, :] == bin_levels[:, None]).astype(
            jnp.float32
        )
        vorticity_table = jnp.where(
            plane_vorticity.reshape(-1)[:, None] == bin_levels[None, :], flat_sensor[:, None], 0.0
        )
        return (
            histogram_totals
            + jnp.dot(dilatation_table, vorticity_table, precision=lax.Precision.HIGHEST),
            None,
        )

    histogram_totals, _ = lax.scan(
        accumulate_plane,
        jnp.zeros((HISTOGRAM_BINS, HISTOGRAM_BINS), jnp.float32),
        (shock_sensor, dilatation_bin, vorticity_bin),
    )
    return histogram_totals


def shards(
    density,
    momentum,
    energy,
    eddy_normal_cell,
    eddy_spanwise_cell,
    eddy_signs,
    eddy_strengths,
    filter_matrices,
    shock_switch,
    dilatation_bin,
    vorticity_bin,
):
    cells_x, span, cells_y = density.shape
    slab_index = lax.axis_index("gx")
    block_index = lax.axis_index("gy")
    slab_count = lax.axis_size("gx")
    fields = jnp.concatenate([density[None], momentum, energy[None]], axis=0)
    total_y = cells_y * lax.axis_size("gy")
    total_eddies = eddy_normal_cell.shape[0] * slab_count
    amplitude = math.sqrt(total_y * span / (total_eddies * SIGMA_Y * SIGMA_Z))
    eddy_weight = (2 * eddy_signs - 1).astype(jnp.float32) * eddy_strengths[:, None] * amplitude
    coords_y = (block_index * cells_y + jnp.arange(cells_y, dtype=jnp.int32)).astype(jnp.float32)
    coords_z = jnp.arange(span, dtype=jnp.int32).astype(jnp.float32)
    partial_sum = inflow_from(
        eddy_normal_cell.astype(jnp.float32),
        eddy_spanwise_cell.astype(jnp.float32),
        eddy_weight,
        coords_y,
        coords_z,
        span,
    )
    inflow = lax.psum(partial_sum, "gx")
    ghost_cells = ghost_state(inflow)
    padded = extended(fields, (("gx", 1), ("gy", 3)), 1)
    padded = padded.at[:, 0, :, 1:-1].set(
        jnp.where(slab_index == 0, ghost_cells, padded[:, 0, :, 1:-1])
    )
    padded = padded.at[:, -1, :, 1:-1].set(
        jnp.where(slab_index == slab_count - 1, fields[:, -1], padded[:, -1, :, 1:-1])
    )
    padded = padded.at[:, 1:-1, :, 0].set(
        jnp.where(block_index == 0, fields[:, :, :, 0], padded[:, 1:-1, :, 0])
    )
    padded = padded.at[:, 1:-1, :, -1].set(
        jnp.where(
            block_index == lax.axis_size("gy") - 1, fields[:, :, :, -1], padded[:, 1:-1, :, -1]
        )
    )
    updated, shock_sensor = section_rhs(padded)
    block_len = filter_matrices.shape[1]
    filter_row = slab_index * cells_x // block_len
    mask_row = lax.dynamic_slice_in_dim(shock_switch, filter_row, 1, 0).astype(jnp.float32)
    weight = mask_row[None] * shock_sensor
    columns = span * cells_y
    stacked = updated.reshape(5, cells_x, columns)
    weight_flat = weight.reshape(1, cells_x, columns)
    pencil, pencil_weight = (
        lax.all_to_all(stacked, "gx", split_axis=2, concat_axis=1, tiled=True),
        lax.all_to_all(weight_flat, "gx", split_axis=2, concat_axis=1, tiled=True),
    )
    smooth = filter_lines(pencil, filter_matrices)
    returned = pencil + pencil_weight * (smooth - pencil)
    back_lines = lax.all_to_all(returned, "gx", split_axis=1, concat_axis=2, tiled=True)
    conserved_next = back_lines.reshape(5, cells_x, span, cells_y)
    partial_histogram = plane_histogram(shock_sensor, dilatation_bin, vorticity_bin)
    summed = lax.psum(partial_histogram, ("gx", "gy"))
    all_cells = cells_x * slab_count * span * total_y
    histogram = summed * (HISTOGRAM_BINS * HISTOGRAM_BINS / all_cells)
    return (conserved_next, histogram)


def solution(mesh):
    in_specs = (
        P("gx", None, "gy"),
        P(None, "gx", None, "gy"),
        P("gx", None, "gy"),
        P("gx"),
        P("gx"),
        P("gx", None),
        P("gx"),
        P(),
        P(None, "gy"),
        P("gx", None, "gy"),
        P("gx", None, "gy"),
    )
    out_specs = (P(None, "gx", None, "gy"), P())
    return jax.shard_map(shards, mesh=mesh, in_specs=in_specs, out_specs=out_specs, check_vma=False)
```

profile of v0, /device:TPU:0, one launch (start us, length us, event | category | flops | bytes accessed | tf_op | source)
XLA Modules:
  0.0 215.9 jit_solution(9551707045615207745)
XLA Ops:
  1.6 1.3 collective-permute-start.1
  2.9 5.5 %collective-permute-start = (f32[5,1,32,32]{3,2,0,1:T(8,128)S(1)}, f32[5,1,32,32]{3,2,0,1:T(8,128)S(1)}, u32[]{:S(2)}, u32[]{:S(2)}) collective-permute-start(f32[5,1,32,32]{3,2,0,1:T(8,128)S(1)} %get-tuple-element.222), channel_id=1, source_target_pairs={{0,2},{2,4},{4,6},{6,8},{8,10},{10,12},{12,14},{14,16},{16,18},{18... | collective-permute-start | bytes 61448 | tf_op jit(solution)/shard_map/ppermute | solution.py:23
  10.8 75.6 %psum.14 = f32[3,32,32]{2,1,0:T(8,128)S(1)} all-reduce(f32[3,32,32]{2,1,0:T(8,128)S(1)} %fusion.50), channel_id=1, replica_groups=mesh['gx'=16,'gy'=2] {'gx'}, use_global_device_ids=true, to_apply=%region_1.2 | all-reduce | flops 3072 | bytes 24576 | tf_op jit(solution)/shard_map/psum | solution.py:153
  91.2 1.3 collective-permute-start.3
  92.5 3.0 %collective-permute-start.2 = (f32[5,10,32,1]{2,3,1,0:T(1,128)S(1)}, f32[5,10,32,1]{2,3,1,0:T(1,128)S(1)}, u32[]{:S(2)}, u32[]{:S(2)}) collective-permute-start(f32[5,10,32,1]{2,3,1,0:T(1,128)S(1)} %copy.81), channel_id=1, source_target_pairs={{0,1},{2,3},{4,5},{6,7},{8,9},{10,11},{12,13},{14,15},{16,17},{18,... | collective-permute-start | bytes 19208 | tf_op jit(solution)/shard_map/ppermute | solution.py:23
  95.5 1.4 and_reduce_fusion
  97.3 1.3 copy.84
  98.6 1.6 pad_maximum_fusion.1
  100.2 1.4 fusion.48
  101.6 1.7 scatter.14
  105.9 3.7 %scatter.19 = f32[5,10,32,34]{3,2,0,1:T(8,128)S(1)} dynamic-update-slice(f32[5,10,32,34]{3,2,0,1:T(8,128)S(1)} %scatter.16, f32[5,8,32,1]{3,2,0,1:T(8,128)S(1)} %slice_select_fusion, s32[]{:T(128)} %constant.328.clone.1, s32[]{:T(128)} %constant.350.clone.1, s32[]{:T(128)} %constant.328.clone.1, s32[]{:T(128)} %constant.351.clone.1) | dynamic-update-slice | bytes 10244 | tf_op jit(solution)/shard_map/scatter | solution.py:165
  114.4 3.7 %reduce.27 = f32[1024,8]{1,0:T(8,128)} reduce(f32[1024,1,8]{2,1,0:T(1,128)} %bitcast.128, f32[]{:T(128)} %broadcast.273), dimensions={1}, to_apply=%bitcast.110.reduce_sub_computation | reduce | bytes 65540
  118.1 1.9 reshape.467
  120.0 3.5 %all-to-all-start.1 = ((f32[16,1,512]{2,1,0:T(1,128)}), f32[16,1,512]{2,1,0:T(1,128)S(1)}, u32[]{:S(2)}, u32[]{:S(2)}) async-start(f32[16,1,512]{2,1,0:T(1,128)} %reshape.467), calls=%async_computation.1 | async-start | bytes 65536 | tf_op jit(solution)/shard_map/all_to_all | solution.py:180
  123.5 2.7 %fusion.14 = f32[5,8,32,32]{3,2,0,1:T(8,128)} fusion(f32[5,10,32,34]{3,2,0,1:T(8,128)S(1)} %get-tuple-element.221, f32[5,10,32,34]{3,2,0,1:T(8,128)S(1)} %scatter.19, f32[5,8,1,32]{3,2,0,1:T(1,128)S(1)} %get-tuple-element.213, f32[5,8,31,32]{3,2,0,1:T(8,128)} %get-tuple-element.215, f32[5,8,31,32]{3,2,0,1:T(8,128)S(1)} %get-tuple-element.214, ...), kind=kLoop, calls=%fused_computation.23 | loop fusion | flops 368640 | bytes 4295680 | tf_op jit(solution)/shard_map/sub | solution.py:75
  126.2 3.6 %copy.122 = f32[5,8,32,32]{1,0,3,2:T(8,128)} copy(f32[5,8,32,32]{3,2,0,1:T(8,128)} %fusion.14) | data formatting | bytes 327680 | tf_op jit(solution)/shard_map/reshape | solution.py:176
  129.8 3.4 %reshape.465 = f32[16,1,2560]{2,1,0:T(1,128)} reshape(f32[1024,5,8]{2,1,0:T(8,128)} %bitcast.117) | data formatting | bytes 327680
  133.1 6.9 %all-to-all-start = ((f32[16,1,2560]{2,1,0:T(1,128)}), f32[16,1,2560]{2,1,0:T(1,128)S(1)}, u32[]{:S(2)}, u32[]{:S(2)}) async-start(f32[16,1,2560]{2,1,0:T(1,128)} %reshape.465), calls=%async_computation | async-start | bytes 327680 | tf_op jit(solution)/shard_map/all_to_all | solution.py:179
  141.8 6.1 %all-to-all-done = f32[16,1,2560]{2,1,0:T(1,128)S(1)} async-done(((f32[16,1,2560]{2,1,0:T(1,128)}), f32[16,1,2560]{2,1,0:T(1,128)S(1)}, u32[]{:S(2)}, u32[]{:S(2)}) %all-to-all-start) | async-done | bytes 163872 | tf_op jit(solution)/shard_map/all_to_all | solution.py:179
  148.9 2.6 %reshape.466 = f32[1024,5,8]{2,1,0:T(8,128)} reshape(f32[16,2560]{1,0:T(8,128)S(1)} %reduce.26) | data formatting | bytes 327680
  151.5 2.6 %copy.103 = f32[5,16,8,64]{3,2,1,0:T(8,128)S(1)} copy(f32[5,16,8,64]{2,0,3,1:T(8,128)} %bitcast.118) | data formatting | bytes 327680 | tf_op jit(solution)/shard_map/all_to_all | solution.py:179
  156.1 3.5 %all-to-all-start.2 = ((f32[16,1,2560]{2,1,0:T(1,128)}), f32[16,1,2560]{2,1,0:T(1,128)S(1)}, u32[]{:S(2)}, u32[]{:S(2)}) async-start(f32[16,1,2560]{2,1,0:T(1,128)} %reshape.469), calls=%async_computation.2 | async-start | bytes 327680 | tf_op jit(solution)/shard_map/all_to_all | solution.py:184
  159.6 12.6 %while.22 = (s32[]{:T(128)}, f32[64,64]{1,0:T(8,128)S(1)}, s32[8,32,32]{2,1,0:T(8,128)}, s32[8,32,32]{2,1,0:T(8,128)}, f32[8,32,32]{2,1,0:T(8,128)S(1)}, /*index=5*/s32[]{:T(128)}, s32[]{:T(128)}) while((s32[]{:T(128)}, f32[64,64]{1,0:T(8,128)S(1)}, s32[8,32,32]{2,1,0:T(8,128)}, s32[8,32,32]{2,1,0:T(8,128)}, ...), condition=%wide.region_4.5_spmd.clone.clone, body=%wide.region_3.4_spmd.clone.clone.sunk | while | flops 50536448 | bytes 94311 | solution.py:113
  172.2 40.8 %psum.15 = f32[64,64]{1,0:T(8,128)S(1)} all-reduce(f32[64,64]{1,0:T(8,128)S(1)} %get-tuple-element.157), channel_id=1, replica_groups=mesh['gx'=16,'gy'=2] {'gx','gy'}, use_global_device_ids=true, to_apply=%region_5.6 | all-reduce | flops 4096 | bytes 32768 | tf_op jit(solution)/shard_map/psum | solution.py:187
  (125 shorter events, 35.6 us)
Async XLA Ops:
  0.6 153.6 %copy-start = (f32[1,128,128]{2,1,0:T(8,128)S(1)}, f32[1,128,128]{2,1,0:T(8,128)}, u32[]{:S(2)}) copy-start(f32[1,128,128]{2,1,0:T(8,128)} %param.40) | copy-start | bytes 196612
  1.6 93.9 %copy-start.4 = (s32[4]{0:T(128)S(1)}, s32[4]{0:T(128)}, u32[]{:S(2)}) copy-start(s32[4]{0:T(128)} %constant.330.clone.1) | copy-start | bytes 52
  1.6 87.3 %collective-permute-start.1 = (f32[5,1,32,32]{3,2,0,1:T(8,128)S(1)}, f32[5,1,32,32]{3,2,0,1:T(8,128)S(1)}, u32[]{:S(2)}, u32[]{:S(2)}) collective-permute-start(f32[5,1,32,32]{3,2,0,1:T(8,128)S(1)} %get-tuple-element.223), channel_id=1, source_target_pairs={{2,0},{4,2},{6,4},{8,6},{10,8},{12,10},{14,12},{16,14},{18,16},{20... | collective-permute-start | bytes 61448 | tf_op jit(solution)/shard_map/ppermute | solution.py:24
  2.9 86.0 %collective-permute-start = (f32[5,1,32,32]{3,2,0,1:T(8,128)S(1)}, f32[5,1,32,32]{3,2,0,1:T(8,128)S(1)}, u32[]{:S(2)}, u32[]{:S(2)}) collective-permute-start(f32[5,1,32,32]{3,2,0,1:T(8,128)S(1)} %get-tuple-element.222), channel_id=1, source_target_pairs={{0,2},{2,4},{4,6},{6,8},{8,10},{10,12},{12,14},{14,16},{16,18},{18... | collective-permute-start | bytes 61448 | tf_op jit(solution)/shard_map/ppermute | solution.py:23
  87.6 11.0 %copy-start.1 = (f32[3,8,32,32]{3,2,1,0:T(8,128)S(1)}, f32[3,8,32,32]{3,2,1,0:T(8,128)}, u32[]{:S(2)}) copy-start(f32[3,8,32,32]{3,2,1,0:T(8,128)} %param.34) | copy-start | bytes 294916
  87.6 11.0 %copy-start.2 = (f32[8,32,32]{2,1,0:T(8,128)S(1)}, f32[8,32,32]{2,1,0:T(8,128)}, u32[]{:S(2)}) copy-start(f32[8,32,32]{2,1,0:T(8,128)} %param.35) | copy-start | bytes 98308
  87.6 11.0 %copy-start.3 = (f32[8,32,32]{2,1,0:T(8,128)S(1)}, f32[8,32,32]{2,1,0:T(8,128)}, u32[]{:S(2)}) copy-start(f32[8,32,32]{2,1,0:T(8,128)} %param.33) | copy-start | bytes 98308
  91.2 6.1 %collective-permute-start.3 = (f32[5,10,32,1]{2,3,1,0:T(1,128)S(1)}, f32[5,10,32,1]{2,3,1,0:T(1,128)S(1)}, u32[]{:S(2)}, u32[]{:S(2)}) collective-permute-start(f32[5,10,32,1]{2,3,1,0:T(1,128)S(1)} %copy.82), channel_id=1, source_target_pairs={{1,0},{3,2},{5,4},{7,6},{9,8},{11,10},{13,12},{15,14},{17,16},{19,... | collective-permute-start | bytes 19208 | tf_op jit(solution)/shard_map/ppermute | solution.py:24
  92.5 4.4 %collective-permute-start.2 = (f32[5,10,32,1]{2,3,1,0:T(1,128)S(1)}, f32[5,10,32,1]{2,3,1,0:T(1,128)S(1)}, u32[]{:S(2)}, u32[]{:S(2)}) collective-permute-start(f32[5,10,32,1]{2,3,1,0:T(1,128)S(1)} %copy.81), channel_id=1, source_target_pairs={{0,1},{2,3},{4,5},{6,7},{8,9},{10,11},{12,13},{14,15},{16,17},{18,... | collective-permute-start | bytes 19208 | tf_op jit(solution)/shard_map/ppermute | solution.py:23
  120.0 13.2 %all-to-all-start.1 = ((f32[16,1,512]{2,1,0:T(1,128)}), f32[16,1,512]{2,1,0:T(1,128)S(1)}, u32[]{:S(2)}, u32[]{:S(2)}) async-start(f32[16,1,512]{2,1,0:T(1,128)} %reshape.467), calls=%async_computation.1 | async-start | bytes 65536 | tf_op jit(solution)/shard_map/all_to_all | solution.py:180
  133.1 14.8 %all-to-all-start = ((f32[16,1,2560]{2,1,0:T(1,128)}), f32[16,1,2560]{2,1,0:T(1,128)S(1)}, u32[]{:S(2)}, u32[]{:S(2)}) async-start(f32[16,1,2560]{2,1,0:T(1,128)} %reshape.465), calls=%async_computation | async-start | bytes 327680 | tf_op jit(solution)/shard_map/all_to_all | solution.py:179
  156.1 57.5 %all-to-all-start.2 = ((f32[16,1,2560]{2,1,0:T(1,128)}), f32[16,1,2560]{2,1,0:T(1,128)S(1)}, u32[]{:S(2)}, u32[]{:S(2)}) async-start(f32[16,1,2560]{2,1,0:T(1,128)} %reshape.469), calls=%async_computation.2 | async-start | bytes 327680 | tf_op jit(solution)/shard_map/all_to_all | solution.py:184
where the time goes:
time: 218 us; the launch traced here: 216 us
  blocking collectives  116 us (53%)
  local copies, waits for them, and re-layouts  39.7 us (18%)
  starting transfers between devices  25 us (11%)
  other arithmetic  21.8 us (10%)
  waiting for transfers between devices  6.13 us (3%)
  matrix products  5.55 us (3%)
    psum x1, blocking collectives, shards(): inflow = lax.psum(partial_sum, 'gx')  75.6 us
    psum x1, blocking collectives, shards(): summed = lax.psum(partial_histogram, ('gx', 'gy'))  40.8 us
    unnamed x16, local copies, waits for them, and re-layouts  9.82 us
    ppermute x2, starting transfers between devices, extended(): before = lax.ppermute(last, axis, up)  8.5 us
    all_to_all x1, starting transfers between devices, shards(): lax.all_to_all(stacked, 'gx', split_axis=2, concat_axis=1, tiled=True)  6.88 us
    all_to_all x1, waiting for transfers between devices, shards(): lax.all_to_all(stacked, 'gx', split_axis=2, concat_axis=1, tiled=True)  6.11 us
    dynamic_slice x16, local copies, waits for them, and re-layouts, plane_histogram(): lax.scan(accumulate_plane, jnp.zeros((HISTOGRAM_BINS, HISTOGRAM_BINS), jn...  6 us
    dot_general x8, matrix products, accumulate_plane(): jnp.dot(dilatation_table, vorticity_table, precision=lax.Precision.HIGHEST)  4.61 us
  transfers between devices with their start and end apart: 7, of which 1 were waited for; matrix products, arithmetic and copies ran while one was open for 14% of the time, Pallas kernels for 0%

commit v1 on v0

--- a/solution.py
+++ b/solution.py
@@ -11,6 +11,22 @@
 GAMMA_GAS = 1.4
 SENSOR_EPS = 0.1
 HAT_PEAK = math.sqrt(1.5)
+
+
+def exchange_in_pairs(x, axis, split, join):
+    ways, here = (lax.axis_size(axis), lax.axis_index(axis))
+    width = x.shape[split] // ways
+    shape = list(x.shape)
+    shape[split] = width
+    height = shape[join]
+    shape[join] = height * ways
+    full = jnp.zeros(shape, x.dtype)
+    for mask in range(ways):
+        part = lax.dynamic_slice_in_dim(x, (here ^ mask) * width, width, axis=split)
+        if mask:
+            part = lax.ppermute(part, axis, [(d, d ^ mask) for d in range(ways)])
+        full = lax.dynamic_update_slice_in_dim(full, part, (here ^ mask) * height, axis=join)
+    return full
 
 
 def extended(x, sides, width):
@@ -176,7 +192,7 @@
     stacked = updated.reshape(5, cells_x, columns)
     weight_flat = weight.reshape(1, cells_x, columns)
     pencil, pencil_weight = (
-        lax.all_to_all(stacked, "gx", split_axis=2, concat_axis=1, tiled=True),
+        exchange_in_pairs(stacked, "gx", 2, 1),
         lax.all_to_all(weight_flat, "gx", split_axis=2, concat_axis=1, tiled=True),
     )
     smooth = filter_lines(pencil, filter_matrices)

time: 218 us -> 284 us (1.30)
  starting transfers between devices: 25 us -> 70.8 us
  local copies, waits for them, and re-layouts: 39.7 us -> 54.6 us
  blocking collectives: 116 us -> 119 us
    ppermute x0 -> x15, starting transfers between devices: none -> 54.4 us  [exchange_in_pairs(): part = lax.ppermute(part, axis, [(d, d ^ mask) for d in range(ways)])]
    dynamic_update_slice x0 -> x16, local copies, waits for them, and re-layouts: none -> 18.6 us  [exchange_in_pairs(): lax.dynamic_update_slice_in_dim(full, part, (here ^ mask) * height, axis=...]
    ppermute x0 -> x15, waiting for transfers between devices: none -> 7.89 us  [exchange_in_pairs(): part = lax.ppermute(part, axis, [(d, d ^ mask) for d in range(ways)])]
    all_to_all x1 -> x0, starting transfers between devices: 6.88 us -> none  [shards(): lax.all_to_all(stacked, 'gx', split_axis=2, concat_axis=1, tiled=True)]
    all_to_all x1 -> x0, waiting for transfers between devices: 6.11 us -> none  [shards(): lax.all_to_all(stacked, 'gx', split_axis=2, concat_axis=1, tiled=True)]
    dynamic_slice x16, local copies, waits for them, and re-layouts: 6 us -> 11.7 us  [plane_histogram(): lax.scan(accumulate_plane, jnp.zeros((HISTOGRAM_BINS, HISTOGRAM_BINS), jn...]
    unnamed x16 -> x15, local copies, waits for them, and re-layouts: 9.82 us -> 4.45 us
    all_to_all x3 -> x0, local copies, waits for them, and re-layouts: 3.26 us -> none  [shards(): lax.all_to_all(stacked, 'gx', split_axis=2, concat_axis=1, tiled=True)]
  transfers between devices with their start and end apart: 7 -> 21, of which waited for: 1 -> 5; matrix products, arithmetic and copies ran while one was open for 14% -> 18% of each run, Pallas kernels for 0% -> 0%
where the time goes in v1:
time: 284 us; the launch traced here: 281 us
  blocking collectives  119 us (42%)
  starting transfers between devices  70.8 us (25%)
  local copies, waits for them, and re-layouts  54.6 us (19%)
  other arithmetic  21.6 us (8%)
  waiting for transfers between devices  7.93 us (3%)
  matrix products  5.18 us (2%)
    psum x1, blocking collectives, shards(): inflow = lax.psum(partial_sum, 'gx')  78.3 us
    ppermute x15, starting transfers between devices, exchange_in_pairs(): part = lax.ppermute(part, axis, [(d, d ^ mask) for d in range(ways)])  54.4 us
    psum x1, blocking collectives, shards(): summed = lax.psum(partial_histogram, ('gx', 'gy'))  40.8 us
    dynamic_update_slice x16, local copies, waits for them, and re-layouts, exchange_in_pairs(): lax.dynamic_update_slice_in_dim(full, part, (here ^ mask) * height, axis=...  18.6 us
    dynamic_slice x16, local copies, waits for them, and re-layouts, plane_histogram(): lax.scan(accumulate_plane, jnp.zeros((HISTOGRAM_BINS, HISTOGRAM_BINS), jn...  11.7 us
    ppermute x15, waiting for transfers between devices, exchange_in_pairs(): part = lax.ppermute(part, axis, [(d, d ^ mask) for d in range(ways)])  7.89 us
    ppermute x2, starting transfers between devices, extended(): before = lax.ppermute(last, axis, up)  6.14 us
  transfers between devices with their start and end apart: 21, of which 5 were waited for; matrix products, arithmetic and copies ran while one was open for 18% of the time, Pallas kernels for 0%

profile of v1, /device:TPU:0, one launch (start us, length us, event | category | flops | bytes accessed | tf_op | source)
XLA Modules:
  0.0 280.7 jit_solution(5808303029233289825)
XLA Ops:
  1.6 4.8 %collective-permute-start = (f32[5,1,32,32]{3,2,0,1:T(8,128)S(1)}, f32[5,1,32,32]{3,2,0,1:T(8,128)S(1)}, u32[]{:S(2)}, u32[]{:S(2)}) collective-permute-start(f32[5,1,32,32]{3,2,0,1:T(8,128)S(1)} %get-tuple-element.238), channel_id=1, source_target_pairs={{0,2},{2,4},{4,6},{6,8},{8,10},{10,12},{12,14},{14,16},{16,18},{18... | collective-permute-start | bytes 61448 | tf_op jit(solution)/shard_map/ppermute | solution.py:39
  10.2 78.3 %psum.14 = f32[3,32,32]{2,1,0:T(8,128)S(1)} all-reduce(f32[3,32,32]{2,1,0:T(8,128)S(1)} %fusion.50), channel_id=1, replica_groups=mesh['gx'=16,'gy'=2] {'gx'}, use_global_device_ids=true, to_apply=%region_1.2 | all-reduce | flops 3072 | bytes 24576 | tf_op jit(solution)/shard_map/psum | solution.py:169
  101.8 1.7 scatter.14
  106.1 3.7 %scatter.19 = f32[5,10,32,34]{3,2,0,1:T(8,128)S(1)} dynamic-update-slice(f32[5,10,32,34]{3,2,0,1:T(8,128)S(1)} %scatter.16, f32[5,8,32,1]{3,2,0,1:T(8,128)S(1)} %slice_select_fusion, s32[]{:T(128)} %constant.344.clone.1, s32[]{:T(128)} %constant.365.clone.1, s32[]{:T(128)} %constant.344.clone.1, s32[]{:T(128)} %constant.366.clone.1) | dynamic-update-slice | bytes 10244 | tf_op jit(solution)/shard_map/scatter | solution.py:181
  115.3 3.8 %reduce.26 = f32[1024,8]{1,0:T(8,128)} reduce(f32[1024,1,8]{2,1,0:T(1,128)} %bitcast.118, f32[]{:T(128)} %broadcast.273), dimensions={1}, to_apply=%bitcast.101.reduce_sub_computation | reduce | bytes 65540
  119.0 1.9 reshape.464
  121.0 3.7 %all-to-all-start = ((f32[16,1,512]{2,1,0:T(1,128)}), f32[16,1,512]{2,1,0:T(1,128)S(1)}, u32[]{:S(2)}, u32[]{:S(2)}) async-start(f32[16,1,512]{2,1,0:T(1,128)} %reshape.464), calls=%async_computation | async-start | bytes 65536 | tf_op jit(solution)/shard_map/all_to_all | solution.py:196
  124.7 2.7 fusion.14
  127.4 1.9 copy.183
  133.7 1.6 collective-permute-start.7
  137.2 2.7 collective-permute-start.9
  143.3 2.2 collective-permute-start.11
  145.5 3.4 %collective-permute-start.12 = (f32[5,8,64]{1,2,0:T(8,128)S(1)}, f32[5,8,64]{1,2,0:T(8,128)S(1)}, u32[]{:S(2)}, u32[]{:S(2)}) collective-permute-start(f32[5,8,64]{1,2,0:T(8,128)S(1)} %get-tuple-element.218), channel_id=1, source_target_pairs={{0,18},{2,16},{4,22},{6,20},{8,26},{10,24},{12,30},{14,28},{16,2},... | collective-permute-start | bytes 30728 | tf_op jit(solution)/shard_map/ppermute | solution.py:27
  148.9 2.5 collective-permute-start.13
  151.4 2.7 collective-permute-done.9
  154.1 2.8 %collective-permute-done.10 = f32[5,8,64]{1,2,0:T(8,128)S(1)} collective-permute-done((f32[5,8,64]{1,2,0:T(8,128)S(1)}, f32[5,8,64]{1,2,0:T(8,128)S(1)}, u32[]{:S(2)}, u32[]{:S(2)}) %collective-permute-start.10) | collective-permute-done | bytes 10272 | tf_op jit(solution)/shard_map/ppermute | solution.py:27
  157.0 1.7 collective-permute-start.15
  158.7 17.9 %collective-permute-start.16 = (f32[5,8,64]{1,2,0:T(8,128)S(1)}, f32[5,8,64]{1,2,0:T(8,128)S(1)}, u32[]{:S(2)}, u32[]{:S(2)}) collective-permute-start(f32[5,8,64]{1,2,0:T(8,128)S(1)} %get-tuple-element.214), channel_id=1, source_target_pairs={{0,26},{2,24},{4,30},{6,28},{8,18},{10,16},{12,22},{14,20},{16,10}... | collective-permute-start | bytes 30728 | tf_op jit(solution)/shard_map/ppermute | solution.py:27
  176.6 12.9 %collective-permute-start.17 = (f32[5,8,64]{1,2,0:T(8,128)S(1)}, f32[5,8,64]{1,2,0:T(8,128)S(1)}, u32[]{:S(2)}, u32[]{:S(2)}) collective-permute-start(f32[5,8,64]{1,2,0:T(8,128)S(1)} %get-tuple-element.213), channel_id=1, source_target_pairs={{0,28},{2,30},{4,24},{6,26},{8,20},{10,22},{12,16},{14,18},{16,12}... | collective-permute-start | bytes 30728 | tf_op jit(solution)/shard_map/ppermute | solution.py:27
  189.5 3.0 %collective-permute-start.18 = (f32[5,8,64]{1,2,0:T(8,128)S(1)}, f32[5,8,64]{1,2,0:T(8,128)}, u32[]{:S(2)}, u32[]{:S(2)}) collective-permute-start(f32[5,8,64]{1,2,0:T(8,128)S(1)} %get-tuple-element.212), channel_id=1, source_target_pairs={{0,30},{2,28},{4,26},{6,24},{8,22},{10,20},{12,18},{14,16},{16,14}... | collective-permute-start | bytes 30728 | tf_op jit(solution)/shard_map/ppermute | solution.py:27
  209.3 2.0 dynamic_update_slice.63
  214.6 4.0 %all-to-all-start.1 = ((f32[16,1,2560]{2,1,0:T(1,128)}), f32[16,1,2560]{2,1,0:T(1,128)S(1)}, u32[]{:S(2)}, u32[]{:S(2)}) async-start(f32[16,1,2560]{2,1,0:T(1,128)} %reshape.466), calls=%async_computation.1 | async-start | bytes 327680 | tf_op jit(solution)/shard_map/all_to_all | solution.py:200
  218.6 18.3 %while.22 = (s32[]{:T(128)}, f32[64,64]{1,0:T(8,128)S(1)}, s32[8,32,32]{2,1,0:T(8,128)}, s32[8,32,32]{2,1,0:T(8,128)}, f32[8,32,32]{2,1,0:T(8,128)}, /*index=5*/s32[]{:T(128)}, s32[]{:T(128)}) while((s32[]{:T(128)}, f32[64,64]{1,0:T(8,128)S(1)}, s32[8,32,32]{2,1,0:T(8,128)}, s32[8,32,32]{2,1,0:T(8,128)}, ...), condition=%wide.region_4.5_spmd.clone.clone, body=%wide.region_3.4_spmd.clone.clone.sunk | while | flops 50536448 | bytes 94303 | solution.py:129
  236.9 40.8 %psum.15 = f32[64,64]{1,0:T(8,128)S(1)} all-reduce(f32[64,64]{1,0:T(8,128)S(1)} %get-tuple-element.157), channel_id=1, replica_groups=mesh['gx'=16,'gy'=2] {'gx','gy'}, use_global_device_ids=true, to_apply=%region_5.6 | all-reduce | flops 4096 | bytes 32768 | tf_op jit(solution)/shard_map/psum | solution.py:203
  (166 shorter events, 76.4 us)
Async XLA Ops:
  0.6 212.5 %copy-start = (f32[1,128,128]{2,1,0:T(8,128)S(1)}, f32[1,128,128]{2,1,0:T(8,128)}, u32[]{:S(2)}) copy-start(f32[1,128,128]{2,1,0:T(8,128)} %param.40) | copy-start | bytes 196612
  0.6 90.3 %copy-start.1 = (f32[3,8,32,32]{3,2,1,0:T(8,128)S(1)}, f32[3,8,32,32]{3,2,1,0:T(8,128)}, u32[]{:S(2)}) copy-start(f32[3,8,32,32]{3,2,1,0:T(8,128)} %param.34) | copy-start | bytes 294916
  1.6 89.4 %collective-permute-start = (f32[5,1,32,32]{3,2,0,1:T(8,128)S(1)}, f32[5,1,32,32]{3,2,0,1:T(8,128)S(1)}, u32[]{:S(2)}, u32[]{:S(2)}) collective-permute-start(f32[5,1,32,32]{3,2,0,1:T(8,128)S(1)} %get-tuple-element.238), channel_id=1, source_target_pairs={{0,2},{2,4},{4,6},{6,8},{8,10},{10,12},{12,14},{14,16},{16,18},{18... | collective-permute-start | bytes 61448 | tf_op jit(solution)/shard_map/ppermute | solution.py:39
  6.5 84.5 %collective-permute-start.1 = (f32[5,1,32,32]{3,2,0,1:T(8,128)S(1)}, f32[5,1,32,32]{3,2,0,1:T(8,128)S(1)}, u32[]{:S(2)}, u32[]{:S(2)}) collective-permute-start(f32[5,1,32,32]{3,2,0,1:T(8,128)S(1)} %get-tuple-element.239), channel_id=1, source_target_pairs={{2,0},{4,2},{6,4},{8,6},{10,8},{12,10},{14,12},{16,14},{18,16},{20... | collective-permute-start | bytes 61448 | tf_op jit(solution)/shard_map/ppermute | solution.py:40
  92.0 6.7 %copy-start.2 = (f32[8,32,32]{2,1,0:T(8,128)S(1)}, f32[8,32,32]{2,1,0:T(8,128)}, u32[]{:S(2)}) copy-start(f32[8,32,32]{2,1,0:T(8,128)} %param.35) | copy-start | bytes 98308
  92.7 4.3 %collective-permute-start.2 = (f32[5,10,32,1]{2,3,1,0:T(1,128)S(1)}, f32[5,10,32,1]{2,3,1,0:T(1,128)S(1)}, u32[]{:S(2)}, u32[]{:S(2)}) collective-permute-start(f32[5,10,32,1]{2,3,1,0:T(1,128)S(1)} %copy.120), channel_id=1, source_target_pairs={{0,1},{2,3},{4,5},{6,7},{8,9},{10,11},{12,13},{14,15},{16,17},{18,... | collective-permute-start | bytes 19208 | tf_op jit(solution)/shard_map/ppermute | solution.py:39
  94.4 3.1 %collective-permute-start.3 = (f32[5,10,32,1]{2,3,1,0:T(1,128)S(1)}, f32[5,10,32,1]{2,3,1,0:T(1,128)S(1)}, u32[]{:S(2)}, u32[]{:S(2)}) collective-permute-start(f32[5,10,32,1]{2,3,1,0:T(1,128)S(1)} %copy.121), channel_id=1, source_target_pairs={{1,0},{3,2},{5,4},{7,6},{9,8},{11,10},{13,12},{15,14},{17,16},{19,... | collective-permute-start | bytes 19208 | tf_op jit(solution)/shard_map/ppermute | solution.py:40
  121.0 90.3 %all-to-all-start = ((f32[16,1,512]{2,1,0:T(1,128)}), f32[16,1,512]{2,1,0:T(1,128)S(1)}, u32[]{:S(2)}, u32[]{:S(2)}) async-start(f32[16,1,512]{2,1,0:T(1,128)} %reshape.464), calls=%async_computation | async-start | bytes 65536 | tf_op jit(solution)/shard_map/all_to_all | solution.py:196
  130.2 6.9 %collective-permute-start.4 = (f32[5,8,64]{1,2,0:T(8,128)S(1)}, f32[5,8,64]{1,2,0:T(8,128)S(1)}, u32[]{:S(2)}, u32[]{:S(2)}) collective-permute-start(f32[5,8,64]{1,2,0:T(8,128)S(1)} %get-tuple-element.226), channel_id=1, source_target_pairs={{0,2},{2,0},{4,6},{6,4},{8,10},{10,8},{12,14},{14,12},{16,18},{18,... | collective-permute-start | bytes 30728 | tf_op jit(solution)/shard_map/ppermute | solution.py:27
  131.8 9.4 %collective-permute-start.5 = (f32[5,8,64]{1,2,0:T(8,128)S(1)}, f32[5,8,64]{1,2,0:T(8,128)S(1)}, u32[]{:S(2)}, u32[]{:S(2)}) collective-permute-start(f32[5,8,64]{1,2,0:T(8,128)S(1)} %get-tuple-element.225), channel_id=1, source_target_pairs={{0,4},{2,6},{4,0},{6,2},{8,12},{10,14},{12,8},{14,10},{16,20},{18,... | collective-permute-start | bytes 30728 | tf_op jit(solution)/shard_map/ppermute | solution.py:27
  133.3 10.0 %collective-permute-start.6 = (f32[5,8,64]{1,2,0:T(8,128)S(1)}, f32[5,8,64]{1,2,0:T(8,128)S(1)}, u32[]{:S(2)}, u32[]{:S(2)}) collective-permute-start(f32[5,8,64]{1,2,0:T(8,128)S(1)} %get-tuple-element.224), channel_id=1, source_target_pairs={{0,6},{2,4},{4,2},{6,0},{8,14},{10,12},{12,10},{14,8},{16,22},{18,... | collective-permute-start | bytes 30728 | tf_op jit(solution)/shard_map/ppermute | solution.py:27
  133.7 11.8 %collective-permute-start.7 = (f32[5,8,64]{1,2,0:T(8,128)S(1)}, f32[5,8,64]{1,2,0:T(8,128)S(1)}, u32[]{:S(2)}, u32[]{:S(2)}) collective-permute-start(f32[5,8,64]{1,2,0:T(8,128)S(1)} %get-tuple-element.223), channel_id=1, source_target_pairs={{0,8},{2,10},{4,12},{6,14},{8,0},{10,2},{12,4},{14,6},{16,24},{18,... | collective-permute-start | bytes 30728 | tf_op jit(solution)/shard_map/ppermute | solution.py:27
  135.3 13.6 %collective-permute-start.8 = (f32[5,8,64]{1,2,0:T(8,128)S(1)}, f32[5,8,64]{1,2,0:T(8,128)S(1)}, u32[]{:S(2)}, u32[]{:S(2)}) collective-permute-start(f32[5,8,64]{1,2,0:T(8,128)S(1)} %get-tuple-element.222), channel_id=1, source_target_pairs={{0,10},{2,8},{4,14},{6,12},{8,2},{10,0},{12,6},{14,4},{16,26},{18,... | collective-permute-start | bytes 30728 | tf_op jit(solution)/shard_map/ppermute | solution.py:27
  137.2 17.0 %collective-permute-start.9 = (f32[5,8,64]{1,2,0:T(8,128)S(1)}, f32[5,8,64]{1,2,0:T(8,128)S(1)}, u32[]{:S(2)}, u32[]{:S(2)}) collective-permute-start(f32[5,8,64]{1,2,0:T(8,128)S(1)} %get-tuple-element.221), channel_id=1, source_target_pairs={{0,12},{2,14},{4,8},{6,10},{8,4},{10,6},{12,0},{14,2},{16,28},{18,... | collective-permute-start | bytes 30728 | tf_op jit(solution)/shard_map/ppermute | solution.py:27
  141.2 15.7 %collective-permute-start.10 = (f32[5,8,64]{1,2,0:T(8,128)S(1)}, f32[5,8,64]{1,2,0:T(8,128)S(1)}, u32[]{:S(2)}, u32[]{:S(2)}) collective-permute-start(f32[5,8,64]{1,2,0:T(8,128)S(1)} %get-tuple-element.220), channel_id=1, source_target_pairs={{0,14},{2,12},{4,10},{6,8},{8,6},{10,4},{12,2},{14,0},{16,30},{18,... | collective-permute-start | bytes 30728 | tf_op jit(solution)/shard_map/ppermute | solution.py:27
  143.3 15.4 %collective-permute-start.11 = (f32[5,8,64]{1,2,0:T(8,128)S(1)}, f32[5,8,64]{1,2,0:T(8,128)S(1)}, u32[]{:S(2)}, u32[]{:S(2)}) collective-permute-start(f32[5,8,64]{1,2,0:T(8,128)S(1)} %get-tuple-element.219), channel_id=1, source_target_pairs={{0,16},{2,18},{4,20},{6,22},{8,24},{10,26},{12,28},{14,30},{16,0},... | collective-permute-start | bytes 30728 | tf_op jit(solution)/shard_map/ppermute | solution.py:27
  145.5 31.1 %collective-permute-start.12 = (f32[5,8,64]{1,2,0:T(8,128)S(1)}, f32[5,8,64]{1,2,0:T(8,128)S(1)}, u32[]{:S(2)}, u32[]{:S(2)}) collective-permute-start(f32[5,8,64]{1,2,0:T(8,128)S(1)} %get-tuple-element.218), channel_id=1, source_target_pairs={{0,18},{2,16},{4,22},{6,20},{8,26},{10,24},{12,30},{14,28},{16,2},... | collective-permute-start | bytes 30728 | tf_op jit(solution)/shard_map/ppermute | solution.py:27
  148.9 40.6 %collective-permute-start.13 = (f32[5,8,64]{1,2,0:T(8,128)S(1)}, f32[5,8,64]{1,2,0:T(8,128)S(1)}, u32[]{:S(2)}, u32[]{:S(2)}) collective-permute-start(f32[5,8,64]{1,2,0:T(8,128)S(1)} %get-tuple-element.217), channel_id=1, source_target_pairs={{0,20},{2,22},{4,16},{6,18},{8,28},{10,30},{12,24},{14,26},{16,4},... | collective-permute-start | bytes 30728 | tf_op jit(solution)/shard_map/ppermute | solution.py:27
  154.1 50.4 %collective-permute-start.14 = (f32[5,8,64]{1,2,0:T(8,128)}, f32[5,8,64]{1,2,0:T(8,128)S(1)}, u32[]{:S(2)}, u32[]{:S(2)}) collective-permute-start(f32[5,8,64]{1,2,0:T(8,128)} %get-tuple-element.216), channel_id=1, source_target_pairs={{0,22},{2,20},{4,18},{6,16},{8,30},{10,28},{12,26},{14,24},{16,6},... | collective-permute-start | bytes 30728 | tf_op jit(solution)/shard_map/ppermute | solution.py:27
  157.0 48.8 %collective-permute-start.15 = (f32[5,8,64]{1,2,0:T(8,128)S(1)}, f32[5,8,64]{1,2,0:T(8,128)S(1)}, u32[]{:S(2)}, u32[]{:S(2)}) collective-permute-start(f32[5,8,64]{1,2,0:T(8,128)S(1)} %get-tuple-element.215), channel_id=1, source_target_pairs={{0,24},{2,26},{4,28},{6,30},{8,16},{10,18},{12,20},{14,22},{16,8},... | collective-permute-start | bytes 30728 | tf_op jit(solution)/shard_map/ppermute | solution.py:27
  158.7 48.2 %collective-permute-start.16 = (f32[5,8,64]{1,2,0:T(8,128)S(1)}, f32[5,8,64]{1,2,0:T(8,128)S(1)}, u32[]{:S(2)}, u32[]{:S(2)}) collective-permute-start(f32[5,8,64]{1,2,0:T(8,128)S(1)} %get-tuple-element.214), channel_id=1, source_target_pairs={{0,26},{2,24},{4,30},{6,28},{8,18},{10,16},{12,22},{14,20},{16,10}... | collective-permute-start | bytes 30728 | tf_op jit(solution)/shard_map/ppermute | solution.py:27
  176.6 31.5 %collective-permute-start.17 = (f32[5,8,64]{1,2,0:T(8,128)S(1)}, f32[5,8,64]{1,2,0:T(8,128)S(1)}, u32[]{:S(2)}, u32[]{:S(2)}) collective-permute-start(f32[5,8,64]{1,2,0:T(8,128)S(1)} %get-tuple-element.213), channel_id=1, source_target_pairs={{0,28},{2,30},{4,24},{6,26},{8,20},{10,22},{12,16},{14,18},{16,12}... | collective-permute-start | bytes 30728 | tf_op jit(solution)/shard_map/ppermute | solution.py:27
  189.5 19.7 %collective-permute-start.18 = (f32[5,8,64]{1,2,0:T(8,128)S(1)}, f32[5,8,64]{1,2,0:T(8,128)}, u32[]{:S(2)}, u32[]{:S(2)}) collective-permute-start(f32[5,8,64]{1,2,0:T(8,128)S(1)} %get-tuple-element.212), channel_id=1, source_target_pairs={{0,30},{2,28},{4,26},{6,24},{8,22},{10,20},{12,18},{14,16},{16,14}... | collective-permute-start | bytes 30728 | tf_op jit(solution)/shard_map/ppermute | solution.py:27
  214.6 63.7 %all-to-all-start.1 = ((f32[16,1,2560]{2,1,0:T(1,128)}), f32[16,1,2560]{2,1,0:T(1,128)S(1)}, u32[]{:S(2)}, u32[]{:S(2)}) async-start(f32[16,1,2560]{2,1,0:T(1,128)} %reshape.466), calls=%async_computation.1 | async-start | bytes 327680 | tf_op jit(solution)/shard_map/all_to_all | solution.py:200
  (2 other events, 10.4 us)
